TPU v7x, 32 devices: a whole 2x2x4 slice. The times are simulated.
32 devices in a mesh: groups: 2 (over y), section: 2 (over core), sp: 4 (over z), blk: 2 (over x).
Axes of the slice: x: 2, y: 2, z: 4, core: 2. Of those that a mesh axis runs over, the one named last changes fastest.
Arguments:
- latent: float32 [2, 12, 64, 128], P('section', ('groups', 'blk'), 'sp'), parts along dimension 1, may hold values from -6 to 6
- queries: bfloat16 [2, 12, 2, 128, 4096], P('section', ('groups', 'blk'), None, 'sp'), parts along dimension 1
- keys: bfloat16 [2, 12, 2, 128, 4096], P('section', ('groups', 'blk'), None, 'sp'), parts along dimension 1
- values: bfloat16 [2, 12, 2, 128, 4096], P('section', ('groups', 'blk'), None, 'sp'), parts along dimension 1, may hold values from -6 to 6
- head_weight: bfloat16 [2, 64, 4096], P('section'), may hold values from -5 to 5
- step_index: int32 [2, 12], P('section', ('groups', 'blk')), parts along dimension 1, may hold values from 0 to 39, as said below
- skip_flags: int32 [12], P(('groups', 'blk')), parts along dimension 0, may hold values 0 or 1
Outputs:
- velocity: float32 [2, 12, 64, 128], P('section', ('groups', 'blk'), 'sp'), parts along dimension 1
- next_latent: float32 [2, 12, 64, 128], P('section', ('groups', 'blk'), 'sp'), parts along dimension 1
There are 2 independent parts, one for each index of `groups`. A program takes and returns all parts, laid end to end along the dimension named above; an argument that names none is the same for every part. Nothing has to cross between parts.
Inputs may be any that keep to these rules, and one draw needn't show every extreme that they name: `step_index`: row 0 (high-noise section) lies below 25, some videos at 24; row 1 (low-noise section) lies in 25 to 39.
All inputs are finite; a program needn't handle non-finite values. No bound on the sum of `skip_flags` on one device may be relied on, other than what follows from the above.
Results may differ from a plain program's by a relative error of at most 0.0041.
Values may be sent and summed in bfloat16 or wider, within the bound.
No kernel may reach another device: no remote copies, remote signals or barrier semaphores. Data moves between devices by JAX's collectives and lax.ppermute only.
A program may use at most 64 MiB of HBM per device.

v0:
```python
import jax
import jax.numpy as jnp
from jax import lax
from jax.sharding import PartitionSpec as P

HD = 128
CH = 64
STEPS = 40
SWITCH = 25
noise_shift = 12.0
high_guidance = 4.0
low_guidance = 3.0


def shifted(array, axis, by):
    devices = lax.axis_size(axis)
    pairs = [(i, i + by) for i in range(devices) if 0 <= i + by < devices]
    return lax.ppermute(array, axis, pairs)


def noise_level(step_now):
    fraction = 1.0 - step_now.astype(jnp.float32) / STEPS
    return noise_shift * fraction / (1.0 + (noise_shift - 1.0) * fraction)


def attend_heads(query_part, key_part, value_part):
    item_count, length, feature_width = query_part.shape
    head_count = feature_width // HD
    query_view = query_part.reshape(item_count, length, head_count, HD)
    key_view = key_part.reshape(item_count, length, head_count, HD)
    value_view = value_part.reshape(item_count, length, head_count, HD)
    scores = jnp.einsum(
        "iqhd,ikhd->ihqk", query_view, key_view, preferred_element_type=jnp.float32
    ) * HD ** (-0.5)
    row_max = jnp.max(scores, axis=3, keepdims=True)
    exponent = jnp.exp(scores - row_max)
    row_total = jnp.sum(exponent, axis=3, keepdims=True)
    weights = (exponent / row_total).astype(jnp.bfloat16)
    attended = jnp.einsum(
        "ihqk,ikhd->iqhd", weights, value_view, preferred_element_type=jnp.float32
    ).astype(jnp.bfloat16)
    return attended.reshape(item_count, length, feature_width)


def on_device(latent, queries, keys, values, head_weight, step_index, skip_flags):
    section_index = lax.axis_index("section")
    video_count = queries.shape[1]
    token_rows = queries.shape[3]
    feature_all = queries.shape[4]
    items = video_count * 2
    query_local = queries[0].reshape(items, token_rows, feature_all)
    key_local = keys[0].reshape(items, token_rows, feature_all)
    value_local = values[0].reshape(items, token_rows, feature_all)
    weight_local = head_weight[0]
    attended = attend_heads(
        lax.all_to_all(query_local, "sp", split_axis=2, concat_axis=1, tiled=True),
        lax.all_to_all(key_local, "sp", split_axis=2, concat_axis=1, tiled=True),
        lax.all_to_all(value_local, "sp", split_axis=2, concat_axis=1, tiled=True),
    )
    item_count = attended.shape[0]
    returned = lax.all_to_all(attended, "sp", split_axis=1, concat_axis=2, tiled=True)
    projected = lax.dot_general(
        returned, weight_local, (((2,), (1,)), ((), ())), preferred_element_type=jnp.float32
    )
    exchanged = projected.reshape(item_count, token_rows // 2, 2 * CH)
    pass_velocity = exchanged.reshape(video_count, 2, token_rows // 2, 2 * CH)
    conditional = pass_velocity[:, 0]
    unconditional = pass_velocity[:, 1]
    guidance = jnp.where(section_index == 0, jnp.float32(high_guidance), jnp.float32(low_guidance))
    guided = unconditional + guidance * (conditional - unconditional)
    skipping = (section_index == 1) & (skip_flags == 1)
    guided = jnp.where(skipping[:, None, None], conditional, guided)
    step_now = step_index[0]
    step_size = noise_level(step_now + 1) - noise_level(step_now)
    updated = latent[0] + step_size[:, None, None] * guided
    finish_mark = jnp.where(
        (section_index == 0) & (step_now + 1 == SWITCH), jnp.float32(1.0), jnp.float32(0.0)
    )
    arrived, arrived_mark = shifted((updated, finish_mark), "section", 1)
    taking = (section_index == 1) & (arrived_mark > 0.5)
    next_latent = jnp.where(taking[:, None, None], arrived, updated)
    return (guided[None], next_latent[None])


def solution(mesh):
    placed = (
        P("section", ("groups", "blk"), "sp", None),
        P("section", ("groups", "blk"), None, "sp", None),
        P("section", ("groups", "blk"), None, "sp", None),
        P("section", ("groups", "blk"), None, "sp", None),
        P("section", None, None),
        P("section", ("groups", "blk")),
        P(("groups", "blk")),
    )
    return jax.shard_map(
        on_device,
        mesh=mesh,
        in_specs=placed,
        out_specs=(
            P("section", ("groups", "blk"), "sp", None),
            P("section", ("groups", "blk"), "sp", None),
        ),
        check_vma=False,
    )
```

profile of v0, /device:TPU:0, one launch (start us, length us, event | category | flops | bytes accessed | tf_op | source)
XLA Modules:
  0.0 233.9 jit_solution(9079173877737753087)
XLA Ops:
  0.6 8.5 %copy.51 = bf16[6,32,4096]{1,0,2:T(8,128)(2,1)} copy(bf16[6,32,4096]{2,1,0:T(8,128)(2,1)} %bitcast.96) | data formatting | bytes 3145728 | tf_op jit(solution)/shard_map/reshape;squeeze | solution.py:51
  9.1 8.7 %reshape.125 = bf16[4,2,98304]{2,1,0:T(2,128)(2,1)} reshape(bf16[4096,6,32]{2,1,0:T(8,128)(2,1)} %bitcast.84) | data formatting | bytes 3145728
  17.9 6.3 %all-to-all-start = ((bf16[4,2,98304]{2,1,0:T(2,128)(2,1)}), bf16[4,2,98304]{2,1,0:T(2,128)(2,1)S(1)}, u32[]{:S(2)}, u32[]{:S(2)}) async-start(bf16[4,2,98304]{2,1,0:T(2,128)(2,1)} %reshape.125), calls=%async_computation | async-start | bytes 3145728 | tf_op jit(solution)/shard_map/all_to_all | solution.py:56
  24.2 8.4 %copy.54 = bf16[6,32,4096]{1,0,2:T(8,128)(2,1)} copy(bf16[6,32,4096]{2,1,0:T(8,128)(2,1)} %bitcast.97) | data formatting | bytes 3145728 | tf_op jit(solution)/shard_map/reshape;squeeze | solution.py:52
  32.6 8.7 %reshape.123 = bf16[4,2,98304]{2,1,0:T(2,128)(2,1)} reshape(bf16[4096,6,32]{2,1,0:T(8,128)(2,1)} %bitcast.85) | data formatting | bytes 3145728
  41.3 19.8 %all-to-all-done = bf16[4,2,98304]{2,1,0:T(2,128)(2,1)S(1)} async-done(((bf16[4,2,98304]{2,1,0:T(2,128)(2,1)}), bf16[4,2,98304]{2,1,0:T(2,128)(2,1)S(1)}, u32[]{:S(2)}, u32[]{:S(2)}) %all-to-all-start) | async-done | bytes 1572896 | tf_op jit(solution)/shard_map/all_to_all | solution.py:56
  61.1 1.2 copy-done.1
  62.3 4.4 %all-to-all-start.1 = ((bf16[4,2,98304]{2,1,0:T(2,128)(2,1)}), bf16[4,2,98304]{2,1,0:T(2,128)(2,1)}, u32[]{:S(2)}, u32[]{:S(2)}) async-start(bf16[4,2,98304]{2,1,0:T(2,128)(2,1)} %reshape.123), calls=%async_computation.1 | async-start | bytes 3145728 | tf_op jit(solution)/shard_map/all_to_all | solution.py:57
  66.7 8.4 %copy.59 = bf16[6,32,4096]{1,0,2:T(8,128)(2,1)} copy(bf16[6,32,4096]{2,1,0:T(8,128)(2,1)} %bitcast.98) | data formatting | bytes 3145728 | tf_op jit(solution)/shard_map/reshape;squeeze | solution.py:53
  75.1 8.8 %reshape.127 = bf16[4,2,98304]{2,1,0:T(2,128)(2,1)} reshape(bf16[4096,6,32]{2,1,0:T(8,128)(2,1)} %bitcast.86) | data formatting | bytes 3145728
  83.8 19.4 %all-to-all-done.1 = bf16[4,2,98304]{2,1,0:T(2,128)(2,1)} async-done(((bf16[4,2,98304]{2,1,0:T(2,128)(2,1)}), bf16[4,2,98304]{2,1,0:T(2,128)(2,1)}, u32[]{:S(2)}, u32[]{:S(2)}) %all-to-all-start.1) | async-done | bytes 1572896 | tf_op jit(solution)/shard_map/all_to_all | solution.py:57
  103.2 3.7 %all-to-all-start.2 = ((bf16[4,2,98304]{2,1,0:T(2,128)(2,1)}), bf16[4,2,98304]{2,1,0:T(2,128)(2,1)S(1)}, u32[]{:S(2)}, u32[]{:S(2)}) async-start(bf16[4,2,98304]{2,1,0:T(2,128)(2,1)} %reshape.127), calls=%async_computation.2 | async-start | bytes 3145728 | tf_op jit(solution)/shard_map/all_to_all | solution.py:58
  106.9 7.9 %reshape.126 = bf16[4096,6,32]{2,1,0:T(8,128)(2,1)} reshape(bf16[4,2,98304]{2,1,0:T(2,128)(2,1)} %copy-done.1) | data formatting | bytes 3145728
  114.8 9.1 %copy.70 = bf16[6,32,4,1024]{3,2,1,0:T(4,128)(2,1)} copy(bf16[6,32,4,1024]{1,0,3,2:T(8,128)(2,1)} %bitcast.81) | data formatting | bytes 3145728 | tf_op jit(solution)/shard_map/all_to_all | solution.py:56
  123.9 1.9 copy.53
  125.8 1.6 copy.77
  127.4 7.9 %reshape.124 = bf16[4096,6,32]{2,1,0:T(8,128)(2,1)} reshape(bf16[4,2,98304]{2,1,0:T(2,128)(2,1)} %all-to-all-done.1) | data formatting | bytes 3145728
  135.3 9.1 %copy.71 = bf16[6,32,4,1024]{3,2,1,0:T(4,128)(2,1)} copy(bf16[6,32,4,1024]{1,0,3,2:T(8,128)(2,1)} %bitcast.82) | data formatting | bytes 3145728 | tf_op jit(solution)/shard_map/all_to_all | solution.py:57
  144.4 1.9 copy.56
  146.8 1.0 copy-done.2
  147.7 1.2 fusion.5
  148.9 2.5 %fusion.20 = (f32[6,8,128]{2,1,0:T(8,128)S(1)}, f32[6,8,128,128]{2,3,1,0:T(8,128)}) fusion(f32[6,8,128,128]{2,3,1,0:T(8,128)S(1)} %fusion.5), kind=kOutput, calls=%fused_computation.31 | output fusion | flops 3145855 | bytes 6316032 | tf_op jit(solution)/shard_map/sub | solution.py:36
  151.4 6.9 %reshape.128 = bf16[4096,6,32]{2,1,0:T(8,128)(2,1)} reshape(bf16[4,2,98304]{2,1,0:T(2,128)(2,1)S(1)} %all-to-all-done.2) | data formatting | bytes 3145728
  158.4 8.4 %copy.72 = bf16[6,32,4,1024]{3,2,1,0:T(4,128)(2,1)S(1)} copy(bf16[6,32,4,1024]{1,0,3,2:T(8,128)(2,1)} %bitcast.83) | data formatting | bytes 3145728 | tf_op jit(solution)/shard_map/all_to_all | solution.py:58
  167.8 1.4 copy-done.3
  169.9 3.0 %copy.64 = bf16[6,128,1024]{2,0,1:T(8,128)(2,1)} copy(bf16[6,128,1024]{1,2,0:T(8,128)(2,1)S(1)} %bitcast.99) | data formatting | bytes 3145728 | tf_op jit(solution)/shard_map/reshape | solution.py:42
  172.9 5.0 %all-to-all-start.3 = ((bf16[6,128,1024]{2,0,1:T(8,128)(2,1)}), bf16[6,128,1024]{2,0,1:T(8,128)(2,1)S(1)}, u32[]{:S(2)}, u32[]{:S(2)}) async-start(bf16[6,128,1024]{2,0,1:T(8,128)(2,1)} %copy.64), calls=%async_computation.3 | async-start | bytes 4194304 | tf_op jit(solution)/shard_map/all_to_all | solution.py:61
  177.9 1.3 collective-permute-start
  180.0 45.0 %all-to-all-done.3 = bf16[6,128,1024]{2,0,1:T(8,128)(2,1)S(1)} async-done(((bf16[6,128,1024]{2,0,1:T(8,128)(2,1)}), bf16[6,128,1024]{2,0,1:T(8,128)(2,1)S(1)}, u32[]{:S(2)}, u32[]{:S(2)}) %all-to-all-start.3) | async-done | bytes 1572896 | tf_op jit(solution)/shard_map/all_to_all | solution.py:61
  225.0 2.4 %copy.66 = bf16[6,32,4,1024]{3,2,1,0:T(4,128)(2,1)} copy(bf16[6,32,4,1024]{3,0,1,2:T(8,128)(2,1)S(1)} %bitcast.87) | data formatting | bytes 3145728 | tf_op jit(solution)/shard_map/all_to_all | solution.py:61
  227.4 2.8 %all_to_all.58 = bf16[6,32,4096]{2,1,0:T(8,128)(2,1)S(1)} reshape(bf16[6,32,4,1024]{3,2,1,0:T(4,128)(2,1)} %copy.66) | data formatting | bytes 3145728 | tf_op jit(solution)/shard_map/all_to_all | solution.py:61
  231.1 1.3 collective-permute-start.1
  (26 shorter events, 5.2 us)
Async XLA Ops:
  0.6 229.6 %copy-start = (bf16[1,64,4096]{2,1,0:T(8,128)(2,1)S(1)}, bf16[1,64,4096]{2,1,0:T(8,128)(2,1)}, u32[]{:S(2)}) copy-start(bf16[1,64,4096]{2,1,0:T(8,128)(2,1)} %param.11) | copy-start | bytes 1572868
  17.9 43.3 %all-to-all-start = ((bf16[4,2,98304]{2,1,0:T(2,128)(2,1)}), bf16[4,2,98304]{2,1,0:T(2,128)(2,1)S(1)}, u32[]{:S(2)}, u32[]{:S(2)}) async-start(bf16[4,2,98304]{2,1,0:T(2,128)(2,1)} %reshape.125), calls=%async_computation | async-start | bytes 3145728 | tf_op jit(solution)/shard_map/all_to_all | solution.py:56
  61.1 1.2 copy-start.1
  62.3 40.9 %all-to-all-start.1 = ((bf16[4,2,98304]{2,1,0:T(2,128)(2,1)}), bf16[4,2,98304]{2,1,0:T(2,128)(2,1)}, u32[]{:S(2)}, u32[]{:S(2)}) async-start(bf16[4,2,98304]{2,1,0:T(2,128)(2,1)} %reshape.123), calls=%async_computation.1 | async-start | bytes 3145728 | tf_op jit(solution)/shard_map/all_to_all | solution.py:57
  103.2 48.2 %all-to-all-start.2 = ((bf16[4,2,98304]{2,1,0:T(2,128)(2,1)}), bf16[4,2,98304]{2,1,0:T(2,128)(2,1)S(1)}, u32[]{:S(2)}, u32[]{:S(2)}) async-start(bf16[4,2,98304]{2,1,0:T(2,128)(2,1)} %reshape.127), calls=%async_computation.2 | async-start | bytes 3145728 | tf_op jit(solution)/shard_map/all_to_all | solution.py:58
  146.3 1.4 copy-start.2
  167.3 1.9 copy-start.3
  172.9 5.0 %copy-start.5 = (s32[1,3]{1,0:T(1,128)S(1)}, s32[1,3]{1,0:T(1,128)}, u32[]{:S(2)}) copy-start(s32[1,3]{1,0:T(1,128)} %param.12) | copy-start | bytes 40
  172.9 6.3 %copy-start.6 = (s32[3]{0:T(128)S(1)}, s32[3]{0:T(128)}, u32[]{:S(2)}) copy-start(s32[3]{0:T(128)} %param.13) | copy-start | bytes 40
  172.9 52.1 %all-to-all-start.3 = ((bf16[6,128,1024]{2,0,1:T(8,128)(2,1)}), bf16[6,128,1024]{2,0,1:T(8,128)(2,1)S(1)}, u32[]{:S(2)}, u32[]{:S(2)}) async-start(bf16[6,128,1024]{2,0,1:T(8,128)(2,1)} %copy.64), calls=%async_computation.3 | async-start | bytes 4194304 | tf_op jit(solution)/shard_map/all_to_all | solution.py:61
  177.9 2.1 collective-permute-start
  230.3 0.7 copy-start.4
  231.1 2.1 collective-permute-start.1
where the time goes:
time: 236 us; the launch traced here: 234 us
  local copies, waits for them, and re-layouts  120 us (51%)
  waiting for transfers between devices  85.1 us (36%)
  starting transfers between devices  22 us (9%)
  other arithmetic  3.95 us (2%)
  matrix products  2.45 us (1%)
    unnamed x23, local copies, waits for them, and re-layouts  55 us
    all_to_all x1, waiting for transfers between devices, on_device(): lax.all_to_all(attended, 'sp', split_axis=1, concat_axis=2, tiled=True)  45 us
    all_to_all x1, waiting for transfers between devices, on_device(): lax.all_to_all(query_local, 'sp', split_axis=2, concat_axis=1, tiled=True)  19.8 us
    all_to_all x1, waiting for transfers between devices, on_device(): lax.all_to_all(key_local, 'sp', split_axis=2, concat_axis=1, tiled=True)  19.4 us
    all_to_all x2, local copies, waits for them, and re-layouts, on_device(): lax.all_to_all(key_local, 'sp', split_axis=2, concat_axis=1, tiled=True)  11 us
    all_to_all x2, local copies, waits for them, and re-layouts, on_device(): lax.all_to_all(query_local, 'sp', split_axis=2, concat_axis=1, tiled=True)  11 us
    all_to_all x2, local copies, waits for them, and re-layouts, on_device(): lax.all_to_all(value_local, 'sp', split_axis=2, concat_axis=1, tiled=True)  8.94 us
    another operation x1, local copies, waits for them, and re-layouts, on_device(): query_local = queries[0].reshape(items, token_rows, feature_all)  8.47 us
  transfers between devices with their start and end apart: 6, of which 5 were waited for; matrix products, arithmetic and copies ran while one was open for 34% of the time, Pallas kernels for 0%

commit v1 on v0

--- a/solution.py
+++ b/solution.py
@@ -55,7 +55,15 @@
     attended = attend_heads(
         lax.all_to_all(query_local, "sp", split_axis=2, concat_axis=1, tiled=True),
         lax.all_to_all(key_local, "sp", split_axis=2, concat_axis=1, tiled=True),
-        lax.all_to_all(value_local, "sp", split_axis=2, concat_axis=1, tiled=True),
+        jnp.concatenate(
+            lax.all_to_all(
+                jnp.stack(jnp.split(value_local, lax.psum(1, "sp"), axis=2)),
+                "sp",
+                split_axis=0,
+                concat_axis=0,
+            ),
+            axis=1,
+        ),
     )
     item_count = attended.shape[0]
     returned = lax.all_to_all(attended, "sp", split_axis=1, concat_axis=2, tiled=True)

time: 236 us -> 215 us (0.911)
  local copies, waits for them, and re-layouts: 120 us -> 83.3 us
  waiting for transfers between devices: 85.1 us -> 99.4 us
    unnamed x23 -> x19, local copies, waits for them, and re-layouts: 55 us -> 37.3 us
    all_to_all x1, waiting for transfers between devices: 19.8 us -> 33.6 us  [on_device(): lax.all_to_all(query_local, 'sp', split_axis=2, concat_axis=1, tiled=True)]
    all_to_all x2 -> x0, local copies, waits for them, and re-layouts: 8.94 us -> none  [on_device(): lax.all_to_all(value_local, 'sp', split_axis=2, concat_axis=1, tiled=True)]
    another operation x1, local copies, waits for them, and re-layouts: 8.42 us -> 1.51 us  [on_device(): jnp.stack(jnp.split(value_local, lax.psum(1, 'sp'), axis=2))]
  transfers between devices with their start and end apart: 6 -> 6, of which waited for: 5 -> 5; matrix products, arithmetic and copies ran while one was open for 34% -> 28% of each run, Pallas kernels for 0% -> 0%
where the time goes in v1:
time: 215 us; the launch traced here: 214 us
  waiting for transfers between devices  99.4 us (46%)
  local copies, waits for them, and re-layouts  83.3 us (39%)
  starting transfers between devices  22.7 us (11%)
  other arithmetic  5.28 us (2%)
  matrix products  2.45 us (1%)
    all_to_all x1, waiting for transfers between devices, on_device(): lax.all_to_all(attended, 'sp', split_axis=1, concat_axis=2, tiled=True)  45 us
    unnamed x19, local copies, waits for them, and re-layouts  37.3 us
    all_to_all x1, waiting for transfers between devices, on_device(): lax.all_to_all(query_local, 'sp', split_axis=2, concat_axis=1, tiled=True)  33.6 us
    all_to_all x1, waiting for transfers between devices, on_device(): lax.all_to_all(key_local, 'sp', split_axis=2, concat_axis=1, tiled=True)  19.8 us
    all_to_all x2, local copies, waits for them, and re-layouts, on_device(): lax.all_to_all(query_local, 'sp', split_axis=2, concat_axis=1, tiled=True)  8.94 us
    all_to_all x2, local copies, waits for them, and re-layouts, on_device(): lax.all_to_all(key_local, 'sp', split_axis=2, concat_axis=1, tiled=True)  8.94 us
    another operation x1, local copies, waits for them, and re-layouts, on_device(): key_local = keys[0].reshape(items, token_rows, feature_all)  8.47 us
    another operation x1, local copies, waits for them, and re-layouts, on_device(): query_local = queries[0].reshape(items, token_rows, feature_all)  8.41 us
  transfers between devices with their start and end apart: 6, of which 5 were waited for; matrix products, arithmetic and copies ran while one was open for 28% of the time, Pallas kernels for 0%

profile of v1, /device:TPU:0, one launch (start us, length us, event | category | flops | bytes accessed | tf_op | source)
XLA Modules:
  0.0 214.0 jit_solution(7060356717316631545)
XLA Ops:
  0.6 8.5 %copy.57 = bf16[6,32,4096]{1,0,2:T(8,128)(2,1)} copy(bf16[6,32,4096]{2,1,0:T(8,128)(2,1)} %bitcast.98) | data formatting | bytes 3145728 | tf_op jit(solution)/shard_map/reshape;squeeze | solution.py:52
  9.1 8.7 %reshape.122 = bf16[4,2,98304]{2,1,0:T(2,128)(2,1)} reshape(bf16[4096,6,32]{2,1,0:T(8,128)(2,1)} %bitcast.88) | data formatting | bytes 3145728
  17.9 6.3 %all-to-all-start.2 = ((bf16[4,2,98304]{2,1,0:T(2,128)(2,1)}), bf16[4,2,98304]{2,1,0:T(2,128)(2,1)S(1)}, u32[]{:S(2)}, u32[]{:S(2)}) async-start(bf16[4,2,98304]{2,1,0:T(2,128)(2,1)} %reshape.122), calls=%async_computation.2 | async-start | bytes 3145728 | tf_op jit(solution)/shard_map/all_to_all | solution.py:57
  24.2 8.4 %copy.54 = bf16[6,32,4096]{1,0,2:T(8,128)(2,1)} copy(bf16[6,32,4096]{2,1,0:T(8,128)(2,1)} %bitcast.99) | data formatting | bytes 3145728 | tf_op jit(solution)/shard_map/reshape;squeeze | solution.py:51
  32.6 8.7 %reshape.124 = bf16[4,2,98304]{2,1,0:T(2,128)(2,1)} reshape(bf16[4096,6,32]{2,1,0:T(8,128)(2,1)} %bitcast.89) | data formatting | bytes 3145728
  41.3 19.8 %all-to-all-done.2 = bf16[4,2,98304]{2,1,0:T(2,128)(2,1)S(1)} async-done(((bf16[4,2,98304]{2,1,0:T(2,128)(2,1)}), bf16[4,2,98304]{2,1,0:T(2,128)(2,1)S(1)}, u32[]{:S(2)}, u32[]{:S(2)}) %all-to-all-start.2) | async-done | bytes 1572896 | tf_op jit(solution)/shard_map/all_to_all | solution.py:57
  61.1 4.3 %all-to-all-start.1 = ((bf16[4,2,98304]{2,1,0:T(2,128)(2,1)}), bf16[4,2,98304]{2,1,0:T(2,128)(2,1)}, u32[]{:S(2)}, u32[]{:S(2)}) async-start(bf16[4,2,98304]{2,1,0:T(2,128)(2,1)} %reshape.124), calls=%async_computation.1 | async-start | bytes 3145728 | tf_op jit(solution)/shard_map/all_to_all | solution.py:56
  65.5 1.5 slice_bitcast_fusion.3
  67.0 1.4 pad_maximum_fusion
  68.4 33.6 %all-to-all-done.1 = bf16[4,2,98304]{2,1,0:T(2,128)(2,1)} async-done(((bf16[4,2,98304]{2,1,0:T(2,128)(2,1)}), bf16[4,2,98304]{2,1,0:T(2,128)(2,1)}, u32[]{:S(2)}, u32[]{:S(2)}) %all-to-all-start.1) | async-done | bytes 1572896 | tf_op jit(solution)/shard_map/all_to_all | solution.py:56
  102.0 4.5 %all-to-all-start = ((bf16[4,6,32,1024]{3,2,1,0:T(8,128)(2,1)}), bf16[4,6,32,1024]{3,2,1,0:T(8,128)(2,1)}, u32[]{:S(2)}, u32[]{:S(2)}) async-start(bf16[4,6,32,1024]{3,2,1,0:T(8,128)(2,1)} %pad_maximum_fusion), calls=%async_computation | async-start | bytes 3145728 | tf_op jit(solution)/shard_map/all_to_all | solution.py:59
  106.5 7.0 %reshape.123 = bf16[4096,6,32]{2,1,0:T(8,128)(2,1)} reshape(bf16[4,2,98304]{2,1,0:T(2,128)(2,1)S(1)} %all-to-all-done.2) | data formatting | bytes 3145728
  113.5 8.4 %copy.71 = bf16[6,32,4,1024]{3,2,1,0:T(4,128)(2,1)S(1)} copy(bf16[6,32,4,1024]{1,0,3,2:T(8,128)(2,1)} %bitcast.86) | data formatting | bytes 3145728 | tf_op jit(solution)/shard_map/all_to_all | solution.py:57
  122.4 1.6 copy.77
  124.1 7.9 %reshape.125 = bf16[4096,6,32]{2,1,0:T(8,128)(2,1)} reshape(bf16[4,2,98304]{2,1,0:T(2,128)(2,1)} %all-to-all-done.1) | data formatting | bytes 3145728
  131.9 8.4 %copy.70 = bf16[6,32,4,1024]{3,2,1,0:T(4,128)(2,1)S(1)} copy(bf16[6,32,4,1024]{1,0,3,2:T(8,128)(2,1)} %bitcast.87) | data formatting | bytes 3145728 | tf_op jit(solution)/shard_map/all_to_all | solution.py:56
  141.3 1.0 copy-done.1
  142.3 1.2 fusion.5
  143.5 2.4 %fusion.20 = (f32[6,8,128]{2,1,0:T(8,128)S(1)}, f32[6,8,128,128]{2,3,1,0:T(8,128)}) fusion(f32[6,8,128,128]{2,3,1,0:T(8,128)S(1)} %fusion.5), kind=kOutput, calls=%fused_computation.36 | output fusion | flops 3145855 | bytes 6316032 | tf_op jit(solution)/shard_map/sub | solution.py:36
  145.9 1.6 copy.53
  147.9 1.4 copy-done.2
  149.4 0.7 convolution_convert_fusion
  150.1 3.0 %copy.64 = bf16[6,128,1024]{2,0,1:T(8,128)(2,1)} copy(bf16[6,128,1024]{1,2,0:T(8,128)(2,1)S(1)} %bitcast.100) | data formatting | bytes 3145728 | tf_op jit(solution)/shard_map/reshape | solution.py:42
  153.0 5.0 %all-to-all-start.3 = ((bf16[6,128,1024]{2,0,1:T(8,128)(2,1)}), bf16[6,128,1024]{2,0,1:T(8,128)(2,1)S(1)}, u32[]{:S(2)}, u32[]{:S(2)}) async-start(bf16[6,128,1024]{2,0,1:T(8,128)(2,1)} %copy.64), calls=%async_computation.3 | async-start | bytes 4194304 | tf_op jit(solution)/shard_map/all_to_all | solution.py:69
  158.0 1.3 collective-permute-start
  159.3 0.8 collective-permute-done
  160.1 45.0 %all-to-all-done.3 = bf16[6,128,1024]{2,0,1:T(8,128)(2,1)S(1)} async-done(((bf16[6,128,1024]{2,0,1:T(8,128)(2,1)}), bf16[6,128,1024]{2,0,1:T(8,128)(2,1)S(1)}, u32[]{:S(2)}, u32[]{:S(2)}) %all-to-all-start.3) | async-done | bytes 1572896 | tf_op jit(solution)/shard_map/all_to_all | solution.py:69
  205.1 2.4 %copy.66 = bf16[6,32,4,1024]{3,2,1,0:T(4,128)(2,1)} copy(bf16[6,32,4,1024]{3,0,1,2:T(8,128)(2,1)S(1)} %bitcast.90) | data formatting | bytes 3145728 | tf_op jit(solution)/shard_map/all_to_all | solution.py:69
  207.5 2.8 %all_to_all.48 = bf16[6,32,4096]{2,1,0:T(8,128)(2,1)S(1)} reshape(bf16[6,32,4,1024]{3,2,1,0:T(4,128)(2,1)} %copy.66) | data formatting | bytes 3145728 | tf_op jit(solution)/shard_map/all_to_all | solution.py:69
  211.2 1.3 collective-permute-start.1
  212.5 0.7 fusion.17
  213.3 0.7 select_bitcast_fusion
  (22 shorter events, 2.9 us)
Async XLA Ops:
  0.6 209.7 %copy-start = (bf16[1,64,4096]{2,1,0:T(8,128)(2,1)S(1)}, bf16[1,64,4096]{2,1,0:T(8,128)(2,1)}, u32[]{:S(2)}) copy-start(bf16[1,64,4096]{2,1,0:T(8,128)(2,1)} %param.11) | copy-start | bytes 1572868
  17.9 43.3 %all-to-all-start.2 = ((bf16[4,2,98304]{2,1,0:T(2,128)(2,1)}), bf16[4,2,98304]{2,1,0:T(2,128)(2,1)S(1)}, u32[]{:S(2)}, u32[]{:S(2)}) async-start(bf16[4,2,98304]{2,1,0:T(2,128)(2,1)} %reshape.122), calls=%async_computation.2 | async-start | bytes 3145728 | tf_op jit(solution)/shard_map/all_to_all | solution.py:57
  61.1 40.9 %all-to-all-start.1 = ((bf16[4,2,98304]{2,1,0:T(2,128)(2,1)}), bf16[4,2,98304]{2,1,0:T(2,128)(2,1)}, u32[]{:S(2)}, u32[]{:S(2)}) async-start(bf16[4,2,98304]{2,1,0:T(2,128)(2,1)} %reshape.124), calls=%async_computation.1 | async-start | bytes 3145728 | tf_op jit(solution)/shard_map/all_to_all | solution.py:56
  102.0 43.9 %all-to-all-start = ((bf16[4,6,32,1024]{3,2,1,0:T(8,128)(2,1)}), bf16[4,6,32,1024]{3,2,1,0:T(8,128)(2,1)}, u32[]{:S(2)}, u32[]{:S(2)}) async-start(bf16[4,6,32,1024]{3,2,1,0:T(8,128)(2,1)} %pad_maximum_fusion), calls=%async_computation | async-start | bytes 3145728 | tf_op jit(solution)/shard_map/all_to_all | solution.py:59
  140.9 1.4 copy-start.1
  147.5 1.9 copy-start.2
  153.0 5.0 %copy-start.4 = (s32[1,3]{1,0:T(1,128)S(1)}, s32[1,3]{1,0:T(1,128)}, u32[]{:S(2)}) copy-start(s32[1,3]{1,0:T(1,128)} %param.12) | copy-start | bytes 40
  153.0 6.3 %copy-start.5 = (s32[3]{0:T(128)S(1)}, s32[3]{0:T(128)}, u32[]{:S(2)}) copy-start(s32[3]{0:T(128)} %param.13) | copy-start | bytes 40
  153.0 52.1 %all-to-all-start.3 = ((bf16[6,128,1024]{2,0,1:T(8,128)(2,1)}), bf16[6,128,1024]{2,0,1:T(8,128)(2,1)S(1)}, u32[]{:S(2)}, u32[]{:S(2)}) async-start(bf16[6,128,1024]{2,0,1:T(8,128)(2,1)} %copy.64), calls=%async_computation.3 | async-start | bytes 4194304 | tf_op jit(solution)/shard_map/all_to_all | solution.py:69
  158.0 2.1 collective-permute-start
  210.4 0.7 copy-start.3
  211.2 2.1 collective-permute-start.1
